TPU v7x, 32 devices: a whole 2x2x4 slice. The times are simulated.
32 devices in a mesh: dp: 16 (over z, x, core), rep: 2 (over y).
Axes of the slice: x: 2, y: 2, z: 4, core: 2. Of those that a mesh axis runs over, the one named last changes fastest.
Arguments:
- grad_out: bfloat16 [12288, 2048], P('dp', 'rep'), may hold values from -6 to 6
- pre_act: bfloat16 [12288, 3072], P('dp', 'rep'), may hold values from -6 to 6
- up_weight: bfloat16 [3072, 2048], P('rep'), may hold values from -0.125 to 0.125
- down_weight: bfloat16 [2048, 3072], P(None, 'rep'), may hold values from -0.109375 to 0.109375
- slot_counts: int32 [16], P('dp'), may hold values from 384 to 768, as said below
Outputs:
- input_grad: bfloat16 [12288, 2048], P('dp')
- down_grad: float32 [2048, 3072], P('dp', 'rep')
Inputs may be any that keep to these rules, and one draw needn't show every extreme that they name: Row i * 768 + j is live exactly when j < slot_counts[i]; some index has all 768 slots live and some index exactly 384.
All inputs are finite; a program needn't handle non-finite values.
Results may differ from a plain program's by a relative error of at most 0.0049.
Values may be sent and summed in bfloat16 or wider, within the bound.
A program may use at most 128 MiB of HBM per device.

v0:
```python
import jax
import jax.numpy as jnp
from jax import lax
from jax.sharding import PartitionSpec as P


def on_device(grad_out, pre_act, up_weight, down_weight, slot_counts):
    slot_rows = grad_out.shape[0]
    live_rows = (lax.iota(jnp.int32, slot_rows) < slot_counts[0])[:, None]
    grad_full = lax.all_gather(grad_out, "rep", axis=1, tiled=True)
    grad_live = jnp.where(live_rows, grad_full, jnp.zeros_like(grad_full))
    zero_pre = jnp.zeros_like(pre_act)
    hidden = jnp.where(live_rows, jnp.maximum(pre_act, zero_pre), zero_pre)
    data_ranks = lax.axis_size("dp")
    down_sum = lax.psum_scatter(
        lax.dot_general(
            grad_live, hidden, (((0,), (0,)), ((), ())), preferred_element_type=jnp.float32
        ),
        "dp",
        scatter_dimension=0,
        tiled=True,
    )
    down_grad = down_sum / data_ranks
    hidden_grad = jnp.dot(grad_live, down_weight, preferred_element_type=jnp.float32)
    pre_grad = jnp.where(pre_act > 0, hidden_grad, jnp.zeros_like(hidden_grad)).astype(jnp.bfloat16)
    partial_terms = jnp.dot(pre_grad, up_weight, preferred_element_type=jnp.float32)
    input_sum = lax.psum(partial_terms, "rep")
    input_grad = input_sum.astype(jnp.bfloat16)
    return (input_grad, down_grad)


def solution(mesh):
    return jax.shard_map(
        on_device,
        mesh=mesh,
        in_specs=(P("dp", "rep"), P("dp", "rep"), P("rep", None), P(None, "rep"), P("dp")),
        out_specs=(P("dp", None), P("dp", "rep")),
        check_vma=False,
    )
```

profile of v0, /device:TPU:0, one launch (start us, length us, event | category | flops | bytes accessed | tf_op | source)
XLA Modules:
  0.0 245.0 jit_solution(6977455939318011038)
XLA Ops:
  7.2 0.0 all-gather.2.cloned.1.call-start
  7.2 0.7 all-gather.2.cloned.1.call-update
  7.9 0.0 reduce-scatter.2.cloned.1.call-start
  8.6 48.6 %all-gather.2.cloned.1.call-done = bf16[768,2048]{1,0:T(8,128)(2,1)} async-done(((bf16[768,1024]{1,0:T(8,128)(2,1)}), bf16[768,2048]{1,0:T(8,128)(2,1)}) %all-gather.2.cloned.1.call-update) | async-done | bytes 3145744 | tf_op jit(solution)/shard_map/all_gather | solution.py:10
  57.2 10.7 %fusion = f32[2048,1536]{1,0:T(8,128)} fusion(bf16[768,1536]{1,0:T(8,128)(2,1)} %param.6, pred[768]{0:T(1024)(128)(4,1)S(1)} %iota_compare_fusion, bf16[768,2048]{1,0:T(8,128)(2,1)} %all-gather.2.cloned.1.call-done), kind=kOutput, calls=%fused_computation.2 | convolution fusion | flops 4835770368 | bytes 18088704 | tf_op jit(solution)/shard_map/dot_general | solution.py:16
  67.9 0.0 copy-start
  67.9 0.0 reduce-scatter.2.cloned.1.call-update
  67.9 1.9 copy-done
  69.8 19.0 %fusion.5 = f32[768,2048]{1,0:T(8,128)} fusion(bf16[1536,2048]{1,0:T(8,128)(2,1)} %param.7, bf16[768,1536]{1,0:T(8,128)(2,1)} %param.6, bf16[2048,1536]{1,0:T(8,128)(2,1)} %param.8, bf16[768,2048]{1,0:T(8,128)(2,1)S(1)} %copy-done, pred[768]{0:T(1024)(128)(4,1)S(1)} %iota_compare_fusion), kind=kOutput, calls=%fused_computation.7 | convolution fusion | flops 9668788224 | bytes 24380160 | tf_op jit(solution)/shard_map/dot_general | solution.py:26
  88.8 147.3 %all-reduce.1 = bf16[768,2048]{1,0:T(8,128)(2,1)} all-reduce(f32[768,2048]{1,0:T(8,128)} %fusion.5), channel_id=1, replica_groups=mesh['dp'=16,'rep'=2] {'rep'}, use_global_device_ids=true, to_apply=%region_0.1 | all-reduce | flops 1572864 | bytes 9437184 | tf_op jit(solution)/shard_map/psum | solution.py:27
  236.1 0.0 reduce-scatter.2.cloned.1.call-done
  236.1 2.1 broadcast_multiply_fusion
  (1 shorter events, 0.0 us)
Async XLA Ops:
  7.2 50.0 %all-gather.2.cloned.1.call-start = ((), (), s32[]{:S(2)}) async-start(), calls=%async_computation.1 | async-start | bytes 4718592 | tf_op jit(solution)/shard_map/all_gather | solution.py:10
  7.9 228.2 %reduce-scatter.2.cloned.1.call-start = ((), (), s32[]{:S(2)}) async-start(), calls=%async_computation.2 | async-start | bytes 13369344 | tf_op jit(solution)/shard_map/reduce_scatter | solution.py:15
  67.9 1.9 copy-start
Sparse Core Ops, SparseCore 0:
  9.5 47.6 all-gather.1
  68.1 134.9 reduce-scatter.1
where the time goes:
time: 245 us
  blocking collectives  147 us (60%)
  waiting for transfers between devices  49.3 us (20%)
  matrix products  29.7 us (12%)
  between operations  14.7 us (6%)
    psum x1, blocking collectives, on_device(): input_sum = lax.psum(partial_terms, 'rep')  147 us
    all_gather x1, waiting for transfers between devices, on_device(): grad_full = lax.all_gather(grad_out, 'rep', axis=1, tiled=True)  48.6 us
    dot_general x1, matrix products, on_device(): jnp.dot(pre_grad, up_weight, preferred_element_type=jnp.float32)  19 us
    dot_general x1, matrix products, on_device(): lax.dot_general(grad_live, hidden, (((0,), (0,)), ((), ())), preferred_el...  10.7 us
  transfers between devices with their start and end apart: 2, of which 1 were waited for; matrix products, arithmetic and copies ran while one was open for 8% of the time, Pallas kernels for 0%

commit v1 on v0

v1 whole, which is shorter than its diff:
```python
import functools

import jax
import jax.numpy as jnp
from jax import lax
from jax.experimental import pallas as pl
from jax.experimental.pallas import tpu as pltpu
from jax.sharding import PartitionSpec as P

MESH = pl.DeviceIdType.MESH
CHUNK = 128


def tile_of(extent):
    return next(t for t in (512, 384, 256, 128) if extent % t == 0)


def kernel(n_dp, n_rep, counts, grad, pre, up, down, ig_out, dg_out,
           gfull, pre_v, hid, up_v, down_v, terms, from_core, from_x, from_z, part, obuf, pg, dg_v,
           load_sem, g_send, g_recv, p_send, p_recv, c_send, c_recv, x_send, x_recv, z_send, z_recv,
           out_sem, dg_sem):
    rows, d_own = grad.shape
    ff = pre.shape[1]
    d_all = down.shape[0]
    n_z = n_dp // 4
    z_own = n_z // n_rep
    blk = d_all // n_dp
    n_chunks = rows // CHUNK
    ff_tile, d_tile = tile_of(ff), tile_of(d_all)

    me = lax.axis_index("dp")
    rep = lax.axis_index("rep")
    my_z, my_x, my_c = me // 4, (me // 2) % 2, me % 2
    core_peer = {"dp": my_z * 4 + my_x * 2 + (1 - my_c)}
    x_peer = {"dp": my_z * 4 + (1 - my_x) * 2 + my_c}
    rep_peers = [lax.rem(rep + o, n_rep) for o in range(1, n_rep)]

    def z_peer(z):
        return {"dp": z * 4 + my_x * 2 + my_c}

    loads = [
        pltpu.make_async_copy(src, dst, load_sem.at[i])
        for i, (src, dst) in enumerate(
            ((grad, gfull.at[rep]), (pre, pre_v), (down, down_v), (up, up_v)))
    ]
    for load in loads:
        load.start()

    barrier = pltpu.get_barrier_semaphore()
    peers = [{"rep": r} for r in rep_peers] + [core_peer, x_peer]
    peers += [z_peer(lax.rem(my_z + o, n_z)) for o in range(1, n_z)]
    for peer in peers:
        pl.semaphore_signal(barrier, inc=1, device_id=peer, device_id_type=MESH)
    pl.semaphore_wait(barrier, len(peers))

    def rows_of(c):
        return pl.ds(pl.multiple_of(c * CHUNK, CHUNK), CHUNK)

    def grad_copy(c, o, source):
        return pltpu.make_async_remote_copy(
            src_ref=grad.at[rows_of(c)], dst_ref=gfull.at[source, rows_of(c)],
            send_sem=g_send.at[c, o], recv_sem=g_recv.at[c, source],
            device_id={"rep": lax.rem(rep + o, n_rep)}, device_id_type=MESH)

    def part_copy(c, o, source):
        return pltpu.make_async_remote_copy(
            src_ref=part.at[rep, rows_of(c)], dst_ref=part.at[source, rows_of(c)],
            send_sem=p_send.at[c, o], recv_sem=p_recv.at[c, source],
            device_id={"rep": lax.rem(rep + o, n_rep)}, device_id_type=MESH)

    for c in range(n_chunks):
        for o in range(1, n_rep):
            grad_copy(c, o, rep).start()

    loads[1].wait()
    count = counts[0]

    def mask_rows(c, _):
        at = lax.broadcasted_iota(jnp.int32, (CHUNK, ff), 0) + c * CHUNK
        kept = jnp.where(at < count, pre_v[rows_of(c), :].astype(jnp.float32), 0.0)
        kept = jnp.maximum(kept, 0.0)
        hid[rows_of(c), :] = kept.astype(jnp.bfloat16)
        return 0

    lax.fori_loop(0, n_chunks, mask_rows, 0)
    loads[0].wait()

    def core_copy(z):
        return pltpu.make_async_remote_copy(
            src_ref=terms.at[z, 1 - my_c], dst_ref=from_core.at[z],
            send_sem=c_send.at[z], recv_sem=c_recv.at[z],
            device_id=core_peer, device_id_type=MESH)

    def x_copy(z):
        return pltpu.make_async_remote_copy(
            src_ref=from_core.at[z, 1 - my_x], dst_ref=from_x.at[z],
            send_sem=x_send.at[z], recv_sem=x_recv.at[z],
            device_id=x_peer, device_id_type=MESH)

    def z_copy(z, source):
        return pltpu.make_async_remote_copy(
            src_ref=from_x.at[z], dst_ref=from_z.at[source],
            send_sem=z_send.at[z], recv_sem=z_recv.at[source],
            device_id=z_peer(z), device_id_type=MESH)

    def z_at(k):
        return lax.rem(rep * z_own + k, n_z)

    def make_terms(k, _):
        z = z_at(k)
        group = z // z_own
        cols = pl.ds(pl.multiple_of((z - group * z_own) * 4 * blk, 4 * blk), 4 * blk)

        def one(j, _):
            at = pl.ds(pl.multiple_of(j * ff_tile, ff_tile), ff_tile)
            out = lax.dot_general(
                gfull[group, :, cols], hid[:, at], (((0,), (0,)), ((), ())),
                preferred_element_type=jnp.float32).astype(jnp.bfloat16)
            for x in range(2):
                for core in range(2):
                    row = (x * 2 + core) * blk
                    terms[z, core, x, :, at] = out[row:row + blk]
            return 0

        lax.fori_loop(0, ff // ff_tile, one, 0)
        core_copy(z).start()
        return 0

    def add_core(k, _):
        z = z_at(k)
        core_copy(z).wait()
        for x in range(2):
            total = from_core[z, x].astype(jnp.float32) + terms[z, my_c, x].astype(jnp.float32)
            from_core[z, x] = total.astype(jnp.bfloat16)
        x_copy(z).start()
        return 0

    def add_x(k, _):
        z = z_at(k)
        x_copy(z).wait()
        total = from_x[z].astype(jnp.float32) + from_core[z, my_x].astype(jnp.float32)
        from_x[z] = total.astype(jnp.bfloat16)

        @pl.when(z != my_z)
        def _():
            z_copy(z, my_z).start()

        return 0

    def chunk(c, _):
        at_rows = rows_of(c)
        for o in range(1, n_rep):
            grad_copy(c, o, lax.rem(rep + o, n_rep)).wait_recv()

        def hidden_tile(j, _):
            at = pl.ds(pl.multiple_of(j * ff_tile, ff_tile), ff_tile)
            total = jnp.dot(gfull[0, at_rows, :], down_v[:d_own, at],
                            preferred_element_type=jnp.float32)
            for g in range(1, n_rep):
                total += jnp.dot(gfull[g, at_rows, :], down_v[g * d_own:(g + 1) * d_own, at],
                                 preferred_element_type=jnp.float32)
            passed = hid[at_rows, at].astype(jnp.float32) > 0.0
            pg[:, at] = jnp.where(passed, total, 0.0).astype(jnp.bfloat16)
            return 0

        lax.fori_loop(0, ff // ff_tile, hidden_tile, 0)

        def out_tile(j, _):
            at = pl.ds(pl.multiple_of(j * d_tile, d_tile), d_tile)
            part[rep, at_rows, at] = jnp.dot(
                pg[...], up_v[:, at], preferred_element_type=jnp.float32).astype(jnp.bfloat16)
            return 0

        lax.fori_loop(0, d_all // d_tile, out_tile, 0)
        for o in range(1, n_rep):
            part_copy(c, o, rep).start()
        return 0

    lax.fori_loop(0, z_own, make_terms, 0)
    loads[2].wait()
    loads[3].wait()
    third = max(n_chunks // 3, 1)
    lax.fori_loop(0, third, chunk, 0)
    lax.fori_loop(0, z_own, add_core, 0)
    lax.fori_loop(third, 2 * third, chunk, 0)
    lax.fori_loop(0, z_own, add_x, 0)
    lax.fori_loop(2 * third, n_chunks, chunk, 0)
    lax.fori_loop(z_own, n_z, make_terms, 0)
    lax.fori_loop(z_own, n_z, add_core, 0)
    lax.fori_loop(z_own, n_z, add_x, 0)

    def out_copy(c):
        return pltpu.make_async_copy(obuf.at[rows_of(c)], ig_out.at[rows_of(c)], out_sem.at[c])

    def finish(c, _):
        at_rows = rows_of(c)
        for o in range(1, n_rep):
            part_copy(c, o, lax.rem(rep + o, n_rep)).wait_recv()
        total = part[0, at_rows, :].astype(jnp.float32)
        for g in range(1, n_rep):
            total += part[g, at_rows, :].astype(jnp.float32)
        obuf[at_rows, :] = total.astype(jnp.bfloat16)
        out_copy(c).start()
        return 0

    lax.fori_loop(0, n_chunks // 2, finish, 0)

    total = from_x[my_z].astype(jnp.float32)
    for o in range(1, n_z):
        source = lax.rem(my_z + o, n_z)
        z_copy(source, source).wait()
        total += from_z[source].astype(jnp.float32)
    dg_v[...] = total / n_dp
    dg_copy = pltpu.make_async_copy(dg_v, dg_out, dg_sem)
    dg_copy.start()

    lax.fori_loop(n_chunks // 2, n_chunks, finish, 0)
    for c in range(n_chunks):
        for o in range(1, n_rep):
            grad_copy(c, o, rep).wait_send()
            part_copy(c, o, rep).wait_send()
        out_copy(c).wait()
    dg_copy.wait()


def on_device(n_dp, n_rep, grad_out, pre_act, up_weight, down_weight, slot_counts):
    rows, d_own = grad_out.shape
    ff = pre_act.shape[1]
    d_all = down_weight.shape[0]
    n_z = n_dp // 4
    blk = d_all // n_dp
    n_chunks = rows // CHUNK
    any_ref = pl.BlockSpec(memory_space=pl.ANY)
    bf16, dma = jnp.bfloat16, pltpu.SemaphoreType.DMA
    return pl.pallas_call(
        functools.partial(kernel, n_dp, n_rep),
        out_shape=(jax.ShapeDtypeStruct((rows, d_all), bf16),
                   jax.ShapeDtypeStruct((blk, ff), jnp.float32)),
        in_specs=[pl.BlockSpec(memory_space=pltpu.SMEM)] + [any_ref] * 4,
        out_specs=(any_ref, any_ref),
        scratch_shapes=[
            pltpu.VMEM((n_rep, rows, d_own), bf16),
            pltpu.VMEM((rows, ff), bf16),
            pltpu.VMEM((rows, ff), bf16),
            pltpu.VMEM((ff, d_all), bf16),
            pltpu.VMEM((d_all, ff), bf16),
            pltpu.VMEM((n_z, 2, 2, blk, ff), bf16),
            pltpu.VMEM((n_z, 2, blk, ff), bf16),
            pltpu.VMEM((n_z, blk, ff), bf16),
            pltpu.VMEM((n_z, blk, ff), bf16),
            pltpu.VMEM((n_rep, rows, d_all), bf16),
            pltpu.VMEM((rows, d_all), bf16),
            pltpu.VMEM((CHUNK, ff), bf16),
            pltpu.VMEM((blk, ff), jnp.float32),
            dma((4,)),
            dma((n_chunks, n_rep)), dma((n_chunks, n_rep)),
            dma((n_chunks, n_rep)), dma((n_chunks, n_rep)),
            dma((n_z,)), dma((n_z,)), dma((n_z,)), dma((n_z,)), dma((n_z,)), dma((n_z,)),
            dma((n_chunks,)), dma,
        ],
        compiler_params=pltpu.CompilerParams(
            collective_id=0, has_side_effects=True, vmem_limit_bytes=63 * 2**20),
    )(slot_counts, grad_out, pre_act, up_weight, down_weight)


def solution(mesh):
    sizes = dict(mesh.shape)
    return jax.shard_map(
        functools.partial(on_device, sizes["dp"], sizes["rep"]),
        mesh=mesh,
        in_specs=(P("dp", "rep"), P("dp", "rep"), P("rep", None), P(None, "rep"), P("dp")),
        out_specs=(P("dp", None), P("dp", "rep")),
        check_vma=False,
    )
```

time: 245 us -> 116 us (0.47)
  blocking collectives: 147 us -> 0 us
  Pallas kernels: 0 us -> 110 us
  waiting for transfers between devices: 49.3 us -> 0 us
  matrix products: 29.7 us -> 0 us
  between operations: 14.7 us -> 1.29 us
  local copies, waits for them, and re-layouts: 1.86 us -> 4.93 us
    psum x1 -> x0, blocking collectives: 147 us -> none  [on_device(): input_sum = lax.psum(partial_terms, 'rep')]
    pallas_call x0 -> x1, Pallas kernels: none -> 110 us  [on_device(): pl.pallas_call(functools.partial(kernel, n_dp, n_rep), out_shape=(jax.Sha...]
    all_gather x1 -> x0, waiting for transfers between devices: 48.6 us -> none  [on_device(): grad_full = lax.all_gather(grad_out, 'rep', axis=1, tiled=True)]
    dot_general x2 -> x0, matrix products: 29.7 us -> none  [the longest x1 19 us: on_device(): jnp.dot(pre_grad, up_weight, preferred_element_type=jnp.float32)]
    unnamed x2 -> x4, local copies, waits for them, and re-layouts: 1.86 us -> 4.93 us
  transfers between devices with their start and end apart: 2 -> 0, of which waited for: 1 -> 0; matrix products, arithmetic and copies ran while one was open for 8% -> 0% of each run, Pallas kernels for 0% -> 0%
where the time goes in v1:
time: 116 us
  Pallas kernels  110 us (95%)
  local copies, waits for them, and re-layouts  4.93 us (4%)
  between operations  1.29 us (1%)
    pallas_call x1, Pallas kernels, on_device(): pl.pallas_call(functools.partial(kernel, n_dp, n_rep), out_shape=(jax.Sha...  110 us
    unnamed x4, local copies, waits for them, and re-layouts  4.93 us

profile of v1, /device:TPU:0, one launch (start us, length us, event | category | flops | bytes accessed | tf_op | source)
XLA Modules:
  0.0 116.3 jit_solution(10753051517173020453)
XLA Ops:
  1.3 110.1 %shard_map.68 = (bf16[768,2048]{1,0:T(8,128)(2,1)}, f32[128,1536]{1,0:T(8,128)}) custom-call(s32[1]{0:T(128)S(6)} %copy.9.counts, bf16[768,1024]{1,0:T(8,128)(2,1)} %grad.1, bf16[768,1536]{1,0:T(8,128)(2,1)} %pre.1, bf16[1536,2048]{1,0:T(8,128)(2,1)} %up.1, bf16[2048,1536]{1,0:T(8,128)(2,1)} %down.1), custom_call_target="tpu_custom_call" | custom-call | tf_op jit(solution)/shard_map/pallas_call | solution.py:235
  111.4 0.0 copy-start
  111.4 4.0 %copy.10 = bf16[768,2048]{1,0:T(8,128)(2,1)} copy(bf16[768,2048]{1,0:T(8,128)(2,1)} %get-tuple-element.4) | data formatting | bytes 6291456
  115.4 0.0 copy-done
  115.4 0.9 copy.11
Async XLA Ops:
  111.4 4.1 %copy-start = (f32[128,1536]{1,0:T(8,128)S(1)}, f32[128,1536]{1,0:T(8,128)}, u32[]{:S(2)}) copy-start(f32[128,1536]{1,0:T(8,128)} %get-tuple-element.5) | copy-start | bytes 2359300

commit v2 on v1

--- a/solution.py
+++ b/solution.py
@@ -16,8 +16,8 @@
 
 
 def kernel(n_dp, n_rep, counts, grad, pre, up, down, ig_out, dg_out,
-           gfull, pre_v, hid, up_v, down_v, terms, from_core, from_x, from_z, part, obuf, pg, dg_v,
-           load_sem, g_send, g_recv, p_send, p_recv, c_send, c_recv, x_send, x_recv, z_send, z_recv,
+           gfull, pre_v, hid, up_all, down_v, terms, from_core, from_x, from_z, masked, own_sum, other_sum, obuf, dg_v,
+           load_sem, g_send, g_recv, p_send, p_recv, uy_send, u_send, u_recv, c_send, c_recv, x_send, x_recv, z_send, z_recv,
            out_sem, dg_sem):
     rows, d_own = grad.shape
     ff = pre.shape[1]
@@ -27,6 +27,11 @@
     blk = d_all // n_dp
     n_chunks = rows // CHUNK
     ff_tile, d_tile = tile_of(ff), tile_of(d_all)
+    slice_rows = n_dp
+    while ff % (slice_rows * 16):
+        slice_rows //= 2
+    slice_cols = n_dp // slice_rows
+    tall, wide = ff // slice_rows, d_all // slice_cols
 
     me = lax.axis_index("dp")
     rep = lax.axis_index("rep")
@@ -41,7 +46,7 @@
     loads = [
         pltpu.make_async_copy(src, dst, load_sem.at[i])
         for i, (src, dst) in enumerate(
-            ((grad, gfull.at[rep]), (pre, pre_v), (down, down_v), (up, up_v)))
+            ((grad, gfull.at[rep]), (pre, pre_v), (down, down_v), (up, up_all.at[rep])))
     ]
     for load in loads:
         load.start()
@@ -64,10 +69,45 @@
 
     def part_copy(c, o, source):
         return pltpu.make_async_remote_copy(
-            src_ref=part.at[rep, rows_of(c)], dst_ref=part.at[source, rows_of(c)],
+            src_ref=masked.at[rep, rows_of(c)], dst_ref=masked.at[source, rows_of(c)],
             send_sem=p_send.at[c, o], recv_sem=p_recv.at[c, source],
             device_id={"rep": lax.rem(rep + o, n_rep)}, device_id_type=MESH)
 
+    def slice_at(s):
+        down_at = pl.ds(pl.multiple_of((s // slice_cols) * tall, tall), tall)
+        if slice_cols == 1:
+            return (down_at,)
+        return (down_at, pl.ds(pl.multiple_of((s % slice_cols) * wide, wide), wide))
+
+    def up_rep_copy(o, source):
+        return pltpu.make_async_remote_copy(
+            src_ref=up.at[slice_at(me)], dst_ref=up_all.at[(source,) + slice_at(me)],
+            send_sem=uy_send.at[o], recv_sem=u_recv.at[source, me],
+            device_id={"rep": lax.rem(rep + o, n_rep)}, device_id_type=MESH)
+
+    def up_copy(g, s, stage, peer):
+        block = up_all.at[(g,) + slice_at(s)]
+        return pltpu.make_async_remote_copy(
+            src_ref=block, dst_ref=block, send_sem=u_send.at[g, stage], recv_sem=u_recv.at[g, s],
+            device_id=peer, device_id_type=MESH)
+
+    def index_of(z, x, core):
+        return z * 4 + x * 2 + core
+
+    def over_z(g, z):
+        return up_copy(g, me, z, z_peer(z))
+
+    def over_x(g, z):
+        return up_copy(g, index_of(z, my_x, my_c), n_z + z, x_peer)
+
+    def over_core(g, z, x):
+        return up_copy(g, index_of(z, x, my_c), 2 * n_z + 2 * z + x, core_peer)
+
+    def landed(g, s):
+        up_copy(g, s, 0, core_peer).wait_recv()
+
+    for o in range(1, n_rep):
+        up_rep_copy(o, rep).start()
     for c in range(n_chunks):
         for o in range(1, n_rep):
             grad_copy(c, o, rep).start()
@@ -160,34 +200,81 @@
                 total += jnp.dot(gfull[g, at_rows, :], down_v[g * d_own:(g + 1) * d_own, at],
                                  preferred_element_type=jnp.float32)
             passed = hid[at_rows, at].astype(jnp.float32) > 0.0
-            pg[:, at] = jnp.where(passed, total, 0.0).astype(jnp.bfloat16)
+            masked[rep, at_rows, at] = jnp.where(passed, total, 0.0).astype(jnp.bfloat16)
             return 0
 
         lax.fori_loop(0, ff // ff_tile, hidden_tile, 0)
 
-        def out_tile(j, _):
-            at = pl.ds(pl.multiple_of(j * d_tile, d_tile), d_tile)
-            part[rep, at_rows, at] = jnp.dot(
-                pg[...], up_v[:, at], preferred_element_type=jnp.float32).astype(jnp.bfloat16)
-            return 0
-
-        lax.fori_loop(0, d_all // d_tile, out_tile, 0)
         for o in range(1, n_rep):
             part_copy(c, o, rep).start()
+        if n_rep == 2:
+            def own_tile(j, _):
+                at = pl.ds(pl.multiple_of(j * d_tile, d_tile), d_tile)
+                own_sum[at_rows, at] = jnp.dot(masked[rep, at_rows, :], up_all[rep, :, at],
+                                               preferred_element_type=jnp.float32)
+                return 0
+
+            lax.fori_loop(0, d_all // d_tile, own_tile, 0)
+        return 0
+
+    def spread_start():
+        for g in rep_peers:
+            landed(g, me)
+            over_x(g, my_z).start()
+            over_core(g, my_z, my_x).start()
+            for o in range(1, n_z):
+                over_z(g, lax.rem(my_z + o, n_z)).start()
+
+    def spread_x(o, _):
+        z = lax.rem(my_z + o, n_z)
+        for g in rep_peers:
+            landed(g, index_of(z, my_x, my_c))
+            over_x(g, z).start()
+            over_core(g, z, my_x).start()
+        return 0
+
+    def spread_core(o, _):
+        z = lax.rem(my_z + o, n_z)
+        for g in rep_peers:
+            landed(g, index_of(z, 1 - my_x, my_c))
+            over_core(g, z, 1 - my_x).start()
+        return 0
+
+    def spread_end(z, _):
+        for g in rep_peers:
+            for x in range(2):
+                landed(g, index_of(z, x, 1 - my_c))
+        return 0
+
+    def spread_sent(z, _):
+        for g in rep_peers:
+            over_x(g, z).wait_send()
+            for x in range(2):
+                over_core(g, z, x).wait_send()
+
+            @pl.when(z != my_z)
+            def _():
+                over_z(g, z).wait_send()
+
         return 0
 
     lax.fori_loop(0, z_own, make_terms, 0)
+    spread_start()
+    lax.fori_loop(0, z_own, add_core, 0)
     loads[2].wait()
     loads[3].wait()
     third = max(n_chunks // 3, 1)
     lax.fori_loop(0, third, chunk, 0)
-    lax.fori_loop(0, z_own, add_core, 0)
+    lax.fori_loop(1, 2, spread_x, 0)
+    lax.fori_loop(0, z_own, add_x, 0)
     lax.fori_loop(third, 2 * third, chunk, 0)
-    lax.fori_loop(0, z_own, add_x, 0)
+    lax.fori_loop(2, n_z, spread_x, 0)
     lax.fori_loop(2 * third, n_chunks, chunk, 0)
     lax.fori_loop(z_own, n_z, make_terms, 0)
     lax.fori_loop(z_own, n_z, add_core, 0)
+    lax.fori_loop(0, n_z, spread_core, 0)
     lax.fori_loop(z_own, n_z, add_x, 0)
+    lax.fori_loop(0, n_z, spread_end, 0)
 
     def out_copy(c):
         return pltpu.make_async_copy(obuf.at[rows_of(c)], ig_out.at[rows_of(c)], out_sem.at[c])
@@ -196,10 +283,25 @@
         at_rows = rows_of(c)
         for o in range(1, n_rep):
             part_copy(c, o, lax.rem(rep + o, n_rep)).wait_recv()
-        total = part[0, at_rows, :].astype(jnp.float32)
-        for g in range(1, n_rep):
-            total += part[g, at_rows, :].astype(jnp.float32)
-        obuf[at_rows, :] = total.astype(jnp.bfloat16)
+
+        def out_tile(j, _):
+            at = pl.ds(pl.multiple_of(j * d_tile, d_tile), d_tile)
+
+            def term(g):
+                other_sum[...] = jnp.dot(masked[g, at_rows, :], up_all[g, :, at],
+                                         preferred_element_type=jnp.float32)
+                return other_sum[...]
+
+            if n_rep == 2:
+                total = own_sum[at_rows, at] + term(1 - rep)
+            else:
+                total = term(0)
+                for g in range(1, n_rep):
+                    total += term(g)
+            obuf[at_rows, at] = total.astype(jnp.bfloat16)
+            return 0
+
+        lax.fori_loop(0, d_all // d_tile, out_tile, 0)
         out_copy(c).start()
         return 0
 
@@ -220,6 +322,9 @@
             grad_copy(c, o, rep).wait_send()
             part_copy(c, o, rep).wait_send()
         out_copy(c).wait()
+    for o in range(1, n_rep):
+        up_rep_copy(o, rep).wait_send()
+    lax.fori_loop(0, n_z, spread_sent, 0)
     dg_copy.wait()
 
 
@@ -242,19 +347,21 @@
             pltpu.VMEM((n_rep, rows, d_own), bf16),
             pltpu.VMEM((rows, ff), bf16),
             pltpu.VMEM((rows, ff), bf16),
-            pltpu.VMEM((ff, d_all), bf16),
+            pltpu.VMEM((n_rep, ff, d_all), bf16),
             pltpu.VMEM((d_all, ff), bf16),
             pltpu.VMEM((n_z, 2, 2, blk, ff), bf16),
             pltpu.VMEM((n_z, 2, blk, ff), bf16),
             pltpu.VMEM((n_z, blk, ff), bf16),
             pltpu.VMEM((n_z, blk, ff), bf16),
-            pltpu.VMEM((n_rep, rows, d_all), bf16),
+            pltpu.VMEM((n_rep, rows, ff), bf16),
+            pltpu.VMEM((rows, d_all), jnp.float32),
+            pltpu.VMEM((CHUNK, tile_of(d_all)), jnp.float32),
             pltpu.VMEM((rows, d_all), bf16),
-            pltpu.VMEM((CHUNK, ff), bf16),
             pltpu.VMEM((blk, ff), jnp.float32),
             dma((4,)),
             dma((n_chunks, n_rep)), dma((n_chunks, n_rep)),
             dma((n_chunks, n_rep)), dma((n_chunks, n_rep)),
+            dma((n_rep,)), dma((n_rep, n_dp)), dma((n_rep, n_dp)),
             dma((n_z,)), dma((n_z,)), dma((n_z,)), dma((n_z,)), dma((n_z,)), dma((n_z,)),
             dma((n_chunks,)), dma,
         ],

time: 116 us -> 130 us (1.12)
  the two profiles are of different devices: /device:TPU:0 before, /device:TPU:24 now
where the time goes in v2:
time: 130 us
  Pallas kernels  123 us (95%)
  local copies, waits for them, and re-layouts  4.93 us (4%)
    pallas_call x1, Pallas kernels, on_device(): pl.pallas_call(functools.partial(kernel, n_dp, n_rep), out_shape=(jax.Sha...  123 us
    unnamed x4, local copies, waits for them, and re-layouts  4.93 us

profile of v2, /device:TPU:24, one launch (start us, length us, event | category | flops | bytes accessed | tf_op | source)
XLA Modules:
  0.0 129.7 jit_solution(9518587696284164792)
XLA Ops:
  1.3 123.5 %shard_map.68 = (bf16[768,2048]{1,0:T(8,128)(2,1)}, f32[128,1536]{1,0:T(8,128)}) custom-call(s32[1]{0:T(128)S(6)} %copy.9.counts, bf16[768,1024]{1,0:T(8,128)(2,1)} %grad.1, bf16[768,1536]{1,0:T(8,128)(2,1)} %pre.1, bf16[1536,2048]{1,0:T(8,128)(2,1)} %up.1, bf16[2048,1536]{1,0:T(8,128)(2,1)} %down.1), custom_call_target="tpu_custom_call" | custom-call | tf_op jit(solution)/shard_map/pallas_call | solution.py:340
  124.7 0.0 copy-start
  124.8 4.0 %copy.10 = bf16[768,2048]{1,0:T(8,128)(2,1)} copy(bf16[768,2048]{1,0:T(8,128)(2,1)} %get-tuple-element.4) | data formatting | bytes 6291456
  128.8 0.0 copy-done
  128.8 0.9 copy.11
Async XLA Ops:
  124.7 4.1 %copy-start = (f32[128,1536]{1,0:T(8,128)S(1)}, f32[128,1536]{1,0:T(8,128)}, u32[]{:S(2)}) copy-start(f32[128,1536]{1,0:T(8,128)} %get-tuple-element.5) | copy-start | bytes 2359300

commit v3 on v1

--- a/solution.py
+++ b/solution.py
@@ -16,9 +16,8 @@
 
 
 def kernel(n_dp, n_rep, counts, grad, pre, up, down, ig_out, dg_out,
-           gfull, pre_v, hid, up_v, down_v, terms, from_core, from_x, from_z, part, obuf, pg, dg_v,
-           load_sem, g_send, g_recv, p_send, p_recv, c_send, c_recv, x_send, x_recv, z_send, z_recv,
-           out_sem, dg_sem):
+           gfull, pre_v, hid, up_v, down_v, terms, from_core, from_x, from_z, part, pg,
+           load_sem, g_send, g_recv, p_send, p_recv, c_send, c_recv, x_send, x_recv, z_send, z_recv):
     rows, d_own = grad.shape
     ff = pre.shape[1]
     d_all = down.shape[0]
@@ -189,9 +188,6 @@
     lax.fori_loop(z_own, n_z, add_core, 0)
     lax.fori_loop(z_own, n_z, add_x, 0)
 
-    def out_copy(c):
-        return pltpu.make_async_copy(obuf.at[rows_of(c)], ig_out.at[rows_of(c)], out_sem.at[c])
-
     def finish(c, _):
         at_rows = rows_of(c)
         for o in range(1, n_rep):
@@ -199,8 +195,7 @@
         total = part[0, at_rows, :].astype(jnp.float32)
         for g in range(1, n_rep):
             total += part[g, at_rows, :].astype(jnp.float32)
-        obuf[at_rows, :] = total.astype(jnp.bfloat16)
-        out_copy(c).start()
+        ig_out[at_rows, :] = total.astype(jnp.bfloat16)
         return 0
 
     lax.fori_loop(0, n_chunks // 2, finish, 0)
@@ -210,17 +205,13 @@
         source = lax.rem(my_z + o, n_z)
         z_copy(source, source).wait()
         total += from_z[source].astype(jnp.float32)
-    dg_v[...] = total / n_dp
-    dg_copy = pltpu.make_async_copy(dg_v, dg_out, dg_sem)
-    dg_copy.start()
+    dg_out[...] = total / n_dp
 
     lax.fori_loop(n_chunks // 2, n_chunks, finish, 0)
     for c in range(n_chunks):
         for o in range(1, n_rep):
             grad_copy(c, o, rep).wait_send()
             part_copy(c, o, rep).wait_send()
-        out_copy(c).wait()
-    dg_copy.wait()
 
 
 def on_device(n_dp, n_rep, grad_out, pre_act, up_weight, down_weight, slot_counts):
@@ -234,10 +225,9 @@
     bf16, dma = jnp.bfloat16, pltpu.SemaphoreType.DMA
     return pl.pallas_call(
         functools.partial(kernel, n_dp, n_rep),
-        out_shape=(jax.ShapeDtypeStruct((rows, d_all), bf16),
-                   jax.ShapeDtypeStruct((blk, ff), jnp.float32)),
+        out_shape=(pltpu.VMEM((rows, d_all), bf16), pltpu.VMEM((blk, ff), jnp.float32)),
         in_specs=[pl.BlockSpec(memory_space=pltpu.SMEM)] + [any_ref] * 4,
-        out_specs=(any_ref, any_ref),
+        out_specs=(pl.BlockSpec(memory_space=pltpu.VMEM),) * 2,
         scratch_shapes=[
             pltpu.VMEM((n_rep, rows, d_own), bf16),
             pltpu.VMEM((rows, ff), bf16),
@@ -249,17 +239,14 @@
             pltpu.VMEM((n_z, blk, ff), bf16),
             pltpu.VMEM((n_z, blk, ff), bf16),
             pltpu.VMEM((n_rep, rows, d_all), bf16),
-            pltpu.VMEM((rows, d_all), bf16),
             pltpu.VMEM((CHUNK, ff), bf16),
-            pltpu.VMEM((blk, ff), jnp.float32),
             dma((4,)),
             dma((n_chunks, n_rep)), dma((n_chunks, n_rep)),
             dma((n_chunks, n_rep)), dma((n_chunks, n_rep)),
             dma((n_z,)), dma((n_z,)), dma((n_z,)), dma((n_z,)), dma((n_z,)), dma((n_z,)),
-            dma((n_chunks,)), dma,
         ],
         compiler_params=pltpu.CompilerParams(
-            collective_id=0, has_side_effects=True, vmem_limit_bytes=63 * 2**20),
+            collective_id=0, has_side_effects=True, vmem_limit_bytes=50 * 2**20),
     )(slot_counts, grad_out, pre_act, up_weight, down_weight)
 
 

time: 116 us -> 113 us (0.974)
  local copies, waits for them, and re-layouts: 4.93 us -> 2.55 us
    unnamed x4 -> x2, local copies, waits for them, and re-layouts: 4.93 us -> 2.55 us
where the time goes in v3:
time: 113 us
  Pallas kernels  109 us (96%)
  local copies, waits for them, and re-layouts  2.55 us (2%)
  between operations  1.29 us (1%)
    pallas_call x1, Pallas kernels, on_device(): pl.pallas_call(functools.partial(kernel, n_dp, n_rep), out_shape=(pltpu.V...  109 us
    unnamed x2, local copies, waits for them, and re-layouts  2.55 us

profile of v3, /device:TPU:0, one launch (start us, length us, event | category | flops | bytes accessed | tf_op | source)
XLA Modules:
  0.0 113.1 jit_solution(9969647104671130271)
XLA Ops:
  1.3 109.2 %shard_map.68 = (bf16[768,2048]{1,0:T(8,128)(2,1)S(1)}, f32[128,1536]{1,0:T(8,128)S(1)}) custom-call(s32[1]{0:T(128)S(6)} %copy.11.counts, bf16[768,1024]{1,0:T(8,128)(2,1)} %grad.1, bf16[768,1536]{1,0:T(8,128)(2,1)} %pre.1, bf16[1536,2048]{1,0:T(8,128)(2,1)} %up.1, bf16[2048,1536]{1,0:T(8,128)(2,1)} %down.1), custom_call_target="tpu_custom_call" | custom-call | tf_op jit(solution)/shard_map/pallas_call | solution.py:226
  110.5 1.7 %copy.9 = bf16[768,2048]{1,0:T(8,128)(2,1)} copy(bf16[768,2048]{1,0:T(8,128)(2,1)S(1)} %get-tuple-element.2) | data formatting | bytes 6291456
  112.2 0.9 copy.10

commit v4 on v2

--- a/solution.py
+++ b/solution.py
@@ -16,9 +16,8 @@
 
 
 def kernel(n_dp, n_rep, counts, grad, pre, up, down, ig_out, dg_out,
-           gfull, pre_v, hid, up_all, down_v, terms, from_core, from_x, from_z, masked, own_sum, other_sum, obuf, dg_v,
-           load_sem, g_send, g_recv, p_send, p_recv, uy_send, u_send, u_recv, c_send, c_recv, x_send, x_recv, z_send, z_recv,
-           out_sem, dg_sem):
+           gfull, hid, up_all, down_v, terms, from_core, from_x, from_z, masked, own_sum, other_sum,
+           load_sem, gp_send, gp_recv, g_send, g_recv, p_send, p_recv, uy_send, u_send, u_recv, c_send, c_recv, x_send, x_recv, z_send, z_recv):
     rows, d_own = grad.shape
     ff = pre.shape[1]
     d_all = down.shape[0]
@@ -46,7 +45,7 @@
     loads = [
         pltpu.make_async_copy(src, dst, load_sem.at[i])
         for i, (src, dst) in enumerate(
-            ((grad, gfull.at[rep]), (pre, pre_v), (down, down_v), (up, up_all.at[rep])))
+            ((grad, gfull.at[rep]), (pre, hid), (down, down_v), (up, up_all.at[rep])))
     ]
     for load in loads:
         load.start()
@@ -61,10 +60,19 @@
     def rows_of(c):
         return pl.ds(pl.multiple_of(c * CHUNK, CHUNK), CHUNK)
 
+    last_cols = pl.ds((z_own - 1) * 4 * blk, 4 * blk)
+
     def grad_copy(c, o, source):
         return pltpu.make_async_remote_copy(
-            src_ref=grad.at[rows_of(c)], dst_ref=gfull.at[source, rows_of(c)],
+            src_ref=grad.at[rows_of(c), last_cols], dst_ref=gfull.at[source, rows_of(c), last_cols],
             send_sem=g_send.at[c, o], recv_sem=g_recv.at[c, source],
+            device_id={"rep": lax.rem(rep + o, n_rep)}, device_id_type=MESH)
+
+    def early_copy(part, o, source):
+        cols = pl.ds(part * 4 * blk, 4 * blk)
+        return pltpu.make_async_remote_copy(
+            src_ref=grad.at[:, cols], dst_ref=gfull.at[source, :, cols],
+            send_sem=gp_send.at[o, part], recv_sem=gp_recv.at[source, part],
             device_id={"rep": lax.rem(rep + o, n_rep)}, device_id_type=MESH)
 
     def part_copy(c, o, source):
@@ -108,6 +116,9 @@
 
     for o in range(1, n_rep):
         up_rep_copy(o, rep).start()
+    for part in range(z_own - 1):
+        for o in range(1, n_rep):
+            early_copy(part, o, rep).start()
     for c in range(n_chunks):
         for o in range(1, n_rep):
             grad_copy(c, o, rep).start()
@@ -117,7 +128,7 @@
 
     def mask_rows(c, _):
         at = lax.broadcasted_iota(jnp.int32, (CHUNK, ff), 0) + c * CHUNK
-        kept = jnp.where(at < count, pre_v[rows_of(c), :].astype(jnp.float32), 0.0)
+        kept = jnp.where(at < count, hid[rows_of(c), :].astype(jnp.float32), 0.0)
         kept = jnp.maximum(kept, 0.0)
         hid[rows_of(c), :] = kept.astype(jnp.bfloat16)
         return 0
@@ -144,7 +155,9 @@
             device_id=z_peer(z), device_id_type=MESH)
 
     def z_at(k):
-        return lax.rem(rep * z_own + k, n_z)
+        late = k - z_own
+        other = lax.rem(rep + 1 + lax.rem(late, n_rep - 1), n_rep) * z_own + late // (n_rep - 1)
+        return jnp.where(k < z_own, rep * z_own + k, other)
 
     def make_terms(k, _):
         z = z_at(k)
@@ -258,26 +271,31 @@
 
         return 0
 
+    first_late, last_late = z_own, n_z - (n_rep - 1)
+    third = max(n_chunks // 3, 1)
     lax.fori_loop(0, z_own, make_terms, 0)
+    lax.fori_loop(0, z_own, add_core, 0)
     spread_start()
-    lax.fori_loop(0, z_own, add_core, 0)
+    for part in range(z_own - 1):
+        for o in range(1, n_rep):
+            early_copy(part, o, lax.rem(rep + o, n_rep)).wait_recv()
+    lax.fori_loop(first_late, last_late, make_terms, 0)
+    lax.fori_loop(0, z_own, add_x, 0)
+    lax.fori_loop(first_late, last_late, add_core, 0)
     loads[2].wait()
     loads[3].wait()
-    third = max(n_chunks // 3, 1)
     lax.fori_loop(0, third, chunk, 0)
     lax.fori_loop(1, 2, spread_x, 0)
-    lax.fori_loop(0, z_own, add_x, 0)
     lax.fori_loop(third, 2 * third, chunk, 0)
+    lax.fori_loop(first_late, last_late, add_x, 0)
+    lax.fori_loop(2 * third, n_chunks, chunk, 0)
+    lax.fori_loop(last_late, n_z, make_terms, 0)
+    lax.fori_loop(last_late, n_z, add_core, 0)
     lax.fori_loop(2, n_z, spread_x, 0)
-    lax.fori_loop(2 * third, n_chunks, chunk, 0)
-    lax.fori_loop(z_own, n_z, make_terms, 0)
-    lax.fori_loop(z_own, n_z, add_core, 0)
-    lax.fori_loop(0, n_z, spread_core, 0)
-    lax.fori_loop(z_own, n_z, add_x, 0)
+    lax.fori_loop(0, 2, spread_core, 0)
+    lax.fori_loop(last_late, n_z, add_x, 0)
+    lax.fori_loop(2, n_z, spread_core, 0)
     lax.fori_loop(0, n_z, spread_end, 0)
-
-    def out_copy(c):
-        return pltpu.make_async_copy(obuf.at[rows_of(c)], ig_out.at[rows_of(c)], out_sem.at[c])
 
     def finish(c, _):
         at_rows = rows_of(c)
@@ -298,11 +316,10 @@
                 total = term(0)
                 for g in range(1, n_rep):
                     total += term(g)
-            obuf[at_rows, at] = total.astype(jnp.bfloat16)
+            ig_out[at_rows, at] = total.astype(jnp.bfloat16)
             return 0
 
         lax.fori_loop(0, d_all // d_tile, out_tile, 0)
-        out_copy(c).start()
         return 0
 
     lax.fori_loop(0, n_chunks // 2, finish, 0)
@@ -312,20 +329,19 @@
         source = lax.rem(my_z + o, n_z)
         z_copy(source, source).wait()
         total += from_z[source].astype(jnp.float32)
-    dg_v[...] = total / n_dp
-    dg_copy = pltpu.make_async_copy(dg_v, dg_out, dg_sem)
-    dg_copy.start()
+    dg_out[...] = total / n_dp
 
     lax.fori_loop(n_chunks // 2, n_chunks, finish, 0)
     for c in range(n_chunks):
         for o in range(1, n_rep):
             grad_copy(c, o, rep).wait_send()
             part_copy(c, o, rep).wait_send()
-        out_copy(c).wait()
+    for part in range(z_own - 1):
+        for o in range(1, n_rep):
+            early_copy(part, o, rep).wait_send()
     for o in range(1, n_rep):
         up_rep_copy(o, rep).wait_send()
     lax.fori_loop(0, n_z, spread_sent, 0)
-    dg_copy.wait()
 
 
 def on_device(n_dp, n_rep, grad_out, pre_act, up_weight, down_weight, slot_counts):
@@ -339,13 +355,11 @@
     bf16, dma = jnp.bfloat16, pltpu.SemaphoreType.DMA
     return pl.pallas_call(
         functools.partial(kernel, n_dp, n_rep),
-        out_shape=(jax.ShapeDtypeStruct((rows, d_all), bf16),
-                   jax.ShapeDtypeStruct((blk, ff), jnp.float32)),
+        out_shape=(pltpu.VMEM((rows, d_all), bf16), pltpu.VMEM((blk, ff), jnp.float32)),
         in_specs=[pl.BlockSpec(memory_space=pltpu.SMEM)] + [any_ref] * 4,
-        out_specs=(any_ref, any_ref),
+        out_specs=(pl.BlockSpec(memory_space=pltpu.VMEM),) * 2,
         scratch_shapes=[
             pltpu.VMEM((n_rep, rows, d_own), bf16),
-            pltpu.VMEM((rows, ff), bf16),
             pltpu.VMEM((rows, ff), bf16),
             pltpu.VMEM((n_rep, ff, d_all), bf16),
             pltpu.VMEM((d_all, ff), bf16),
@@ -356,17 +370,14 @@
             pltpu.VMEM((n_rep, rows, ff), bf16),
             pltpu.VMEM((rows, d_all), jnp.float32),
             pltpu.VMEM((CHUNK, tile_of(d_all)), jnp.float32),
-            pltpu.VMEM((rows, d_all), bf16),
-            pltpu.VMEM((blk, ff), jnp.float32),
-            dma((4,)),
+            dma((4,)), dma((n_rep, n_z)), dma((n_rep, n_z)),
             dma((n_chunks, n_rep)), dma((n_chunks, n_rep)),
             dma((n_chunks, n_rep)), dma((n_chunks, n_rep)),
             dma((n_rep,)), dma((n_rep, n_dp)), dma((n_rep, n_dp)),
             dma((n_z,)), dma((n_z,)), dma((n_z,)), dma((n_z,)), dma((n_z,)), dma((n_z,)),
-            dma((n_chunks,)), dma,
         ],
         compiler_params=pltpu.CompilerParams(
-            collective_id=0, has_side_effects=True, vmem_limit_bytes=63 * 2**20),
+            collective_id=0, has_side_effects=True, vmem_limit_bytes=54 * 2**20),
     )(slot_counts, grad_out, pre_act, up_weight, down_weight)
 
 

time: 130 us -> 126 us (0.969)
  the two profiles are of different devices: /device:TPU:24 before, /device:TPU:9 now
where the time goes in v4:
time: 126 us
  Pallas kernels  122 us (97%)
  local copies, waits for them, and re-layouts  2.55 us (2%)
  between operations  1.29 us (1%)
    pallas_call x1, Pallas kernels, on_device(): pl.pallas_call(functools.partial(kernel, n_dp, n_rep), out_shape=(pltpu.V...  122 us
    unnamed x2, local copies, waits for them, and re-layouts  2.55 us

profile of v4, /device:TPU:9, one launch (start us, length us, event | category | flops | bytes accessed | tf_op | source)
XLA Modules:
  0.0 125.7 jit_solution(5722778425900901502)
XLA Ops:
  1.3 121.9 %shard_map.68 = (bf16[768,2048]{1,0:T(8,128)(2,1)S(1)}, f32[128,1536]{1,0:T(8,128)S(1)}) custom-call(s32[1]{0:T(128)S(6)} %copy.11.counts, bf16[768,1024]{1,0:T(8,128)(2,1)} %grad.1, bf16[768,1536]{1,0:T(8,128)(2,1)} %pre.1, bf16[1536,2048]{1,0:T(8,128)(2,1)} %up.1, bf16[2048,1536]{1,0:T(8,128)(2,1)} %down.1), custom_call_target="tpu_custom_call" | custom-call | tf_op jit(solution)/shard_map/pallas_call | solution.py:356
  123.1 1.7 %copy.9 = bf16[768,2048]{1,0:T(8,128)(2,1)} copy(bf16[768,2048]{1,0:T(8,128)(2,1)S(1)} %get-tuple-element.2) | data formatting | bytes 6291456
  124.8 0.9 copy.10

commit v5 on v4

--- a/solution.py
+++ b/solution.py
@@ -102,8 +102,9 @@
     def index_of(z, x, core):
         return z * 4 + x * 2 + core
 
-    def over_z(g, z):
-        return up_copy(g, me, z, z_peer(z))
+    def along_z(g, z, stage, step):
+        to = lax.rem(my_z + step + n_z, n_z)
+        return up_copy(g, index_of(z, my_x, my_c), stage, z_peer(to))
 
     def over_x(g, z):
         return up_copy(g, index_of(z, my_x, my_c), n_z + z, x_peer)
@@ -235,22 +236,46 @@
             landed(g, me)
             over_x(g, my_z).start()
             over_core(g, my_z, my_x).start()
-            for o in range(1, n_z):
-                over_z(g, lax.rem(my_z + o, n_z)).start()
-
-    def spread_x(o, _):
-        z = lax.rem(my_z + o, n_z)
-        for g in rep_peers:
-            landed(g, index_of(z, my_x, my_c))
-            over_x(g, z).start()
-            over_core(g, z, my_x).start()
-        return 0
-
-    def spread_core(o, _):
-        z = lax.rem(my_z + o, n_z)
+
+            @pl.when(my_z + 1 < n_z)
+            def _():
+                along_z(g, my_z, my_z, 1).start()
+
+            @pl.when(my_z > 0)
+            def _():
+                along_z(g, my_z, n_dp, -1).start()
+
+    def both_sides(d, visit):
+        @pl.when(my_z >= d)
+        def _():
+            visit(my_z - d, my_z + 1 < n_z, 1)
+
+        @pl.when(my_z + d < n_z)
+        def _():
+            visit(my_z + d, my_z > 0, -1)
+
+    def spread_x(d, _):
+        def visit(z, goes_on, step):
+            for g in rep_peers:
+                landed(g, index_of(z, my_x, my_c))
+
+                @pl.when(goes_on)
+                def _():
+                    along_z(g, z, z, step).start()
+
+                over_x(g, z).start()
+                over_core(g, z, my_x).start()
+
+        both_sides(d, visit)
+        return 0
+
+    def pass_core(z):
         for g in rep_peers:
             landed(g, index_of(z, 1 - my_x, my_c))
             over_core(g, z, 1 - my_x).start()
+
+    def spread_core(d, _):
+        both_sides(d, lambda z, goes_on, step: pass_core(z))
         return 0
 
     def spread_end(z, _):
@@ -265,9 +290,17 @@
             for x in range(2):
                 over_core(g, z, x).wait_send()
 
-            @pl.when(z != my_z)
+            @pl.when((z <= my_z) & (my_z + 1 < n_z))
             def _():
-                over_z(g, z).wait_send()
+                along_z(g, z, z, 1).wait_send()
+
+            @pl.when((z > my_z) & (my_z > 0))
+            def _():
+                along_z(g, z, z, -1).wait_send()
+
+            @pl.when((z == my_z) & (my_z > 0))
+            def _():
+                along_z(g, z, n_dp, -1).wait_send()
 
         return 0
 
@@ -280,19 +313,21 @@
         for o in range(1, n_rep):
             early_copy(part, o, lax.rem(rep + o, n_rep)).wait_recv()
     lax.fori_loop(first_late, last_late, make_terms, 0)
+    lax.fori_loop(first_late, last_late, add_core, 0)
+    lax.fori_loop(1, 2, spread_x, 0)
     lax.fori_loop(0, z_own, add_x, 0)
-    lax.fori_loop(first_late, last_late, add_core, 0)
     loads[2].wait()
     loads[3].wait()
     lax.fori_loop(0, third, chunk, 0)
-    lax.fori_loop(1, 2, spread_x, 0)
+    lax.fori_loop(first_late, last_late, add_x, 0)
     lax.fori_loop(third, 2 * third, chunk, 0)
-    lax.fori_loop(first_late, last_late, add_x, 0)
+    lax.fori_loop(2, 3, spread_x, 0)
     lax.fori_loop(2 * third, n_chunks, chunk, 0)
     lax.fori_loop(last_late, n_z, make_terms, 0)
     lax.fori_loop(last_late, n_z, add_core, 0)
-    lax.fori_loop(2, n_z, spread_x, 0)
-    lax.fori_loop(0, 2, spread_core, 0)
+    lax.fori_loop(3, n_z, spread_x, 0)
+    pass_core(my_z)
+    lax.fori_loop(1, 2, spread_core, 0)
     lax.fori_loop(last_late, n_z, add_x, 0)
     lax.fori_loop(2, n_z, spread_core, 0)
     lax.fori_loop(0, n_z, spread_end, 0)
@@ -322,7 +357,7 @@
         lax.fori_loop(0, d_all // d_tile, out_tile, 0)
         return 0
 
-    lax.fori_loop(0, n_chunks // 2, finish, 0)
+    lax.fori_loop(0, n_chunks - 1, finish, 0)
 
     total = from_x[my_z].astype(jnp.float32)
     for o in range(1, n_z):
@@ -331,7 +366,7 @@
         total += from_z[source].astype(jnp.float32)
     dg_out[...] = total / n_dp
 
-    lax.fori_loop(n_chunks // 2, n_chunks, finish, 0)
+    lax.fori_loop(n_chunks - 1, n_chunks, finish, 0)
     for c in range(n_chunks):
         for o in range(1, n_rep):
             grad_copy(c, o, rep).wait_send()
@@ -373,7 +408,7 @@
             dma((4,)), dma((n_rep, n_z)), dma((n_rep, n_z)),
             dma((n_chunks, n_rep)), dma((n_chunks, n_rep)),
             dma((n_chunks, n_rep)), dma((n_chunks, n_rep)),
-            dma((n_rep,)), dma((n_rep, n_dp)), dma((n_rep, n_dp)),
+            dma((n_rep,)), dma((n_rep, n_dp + 1)), dma((n_rep, n_dp)),
             dma((n_z,)), dma((n_z,)), dma((n_z,)), dma((n_z,)), dma((n_z,)), dma((n_z,)),
         ],
         compiler_params=pltpu.CompilerParams(

time: 126 us -> 113 us (0.90)
  the two profiles are of different devices: /device:TPU:9 before, /device:TPU:24 now
where the time goes in v5:
time: 113 us; the launch traced here: 112 us
  Pallas kernels  109 us (96%)
  local copies, waits for them, and re-layouts  2.55 us (2%)
  between operations  1.29 us (1%)
    pallas_call x1, Pallas kernels, on_device(): pl.pallas_call(functools.partial(kernel, n_dp, n_rep), out_shape=(pltpu.V...  109 us
    unnamed x2, local copies, waits for them, and re-layouts  2.55 us

profile of v5, /device:TPU:24, one launch (start us, length us, event | category | flops | bytes accessed | tf_op | source)
XLA Modules:
  0.0 112.4 jit_solution(5044513241390635246)
XLA Ops:
  1.3 108.6 %shard_map.68 = (bf16[768,2048]{1,0:T(8,128)(2,1)S(1)}, f32[128,1536]{1,0:T(8,128)S(1)}) custom-call(s32[1]{0:T(128)S(6)} %copy.11.counts, bf16[768,1024]{1,0:T(8,128)(2,1)} %grad.1, bf16[768,1536]{1,0:T(8,128)(2,1)} %pre.1, bf16[1536,2048]{1,0:T(8,128)(2,1)} %up.1, bf16[2048,1536]{1,0:T(8,128)(2,1)} %down.1), custom_call_target="tpu_custom_call" | custom-call | tf_op jit(solution)/shard_map/pallas_call | solution.py:391
  109.9 1.7 %copy.9 = bf16[768,2048]{1,0:T(8,128)(2,1)} copy(bf16[768,2048]{1,0:T(8,128)(2,1)S(1)} %get-tuple-element.2) | data formatting | bytes 6291456
  111.6 0.9 copy.10

commit v6 on v5

--- a/solution.py
+++ b/solution.py
@@ -254,7 +254,7 @@
         def _():
             visit(my_z + d, my_z > 0, -1)
 
-    def spread_x(d, _):
+    def spread_z(d, _):
         def visit(z, goes_on, step):
             for g in rep_peers:
                 landed(g, index_of(z, my_x, my_c))
@@ -263,8 +263,15 @@
                 def _():
                     along_z(g, z, z, step).start()
 
+                over_core(g, z, my_x).start()
+
+        both_sides(d, visit)
+        return 0
+
+    def cross_x(d, _):
+        def visit(z, goes_on, step):
+            for g in rep_peers:
                 over_x(g, z).start()
-                over_core(g, z, my_x).start()
 
         both_sides(d, visit)
         return 0
@@ -314,18 +321,21 @@
             early_copy(part, o, lax.rem(rep + o, n_rep)).wait_recv()
     lax.fori_loop(first_late, last_late, make_terms, 0)
     lax.fori_loop(first_late, last_late, add_core, 0)
-    lax.fori_loop(1, 2, spread_x, 0)
+    lax.fori_loop(1, 2, spread_z, 0)
+    lax.fori_loop(1, 2, cross_x, 0)
     lax.fori_loop(0, z_own, add_x, 0)
     loads[2].wait()
     loads[3].wait()
     lax.fori_loop(0, third, chunk, 0)
     lax.fori_loop(first_late, last_late, add_x, 0)
     lax.fori_loop(third, 2 * third, chunk, 0)
-    lax.fori_loop(2, 3, spread_x, 0)
+    lax.fori_loop(2, 3, spread_z, 0)
     lax.fori_loop(2 * third, n_chunks, chunk, 0)
     lax.fori_loop(last_late, n_z, make_terms, 0)
     lax.fori_loop(last_late, n_z, add_core, 0)
-    lax.fori_loop(3, n_z, spread_x, 0)
+    lax.fori_loop(2, 3, cross_x, 0)
+    lax.fori_loop(3, n_z, spread_z, 0)
+    lax.fori_loop(3, n_z, cross_x, 0)
     pass_core(my_z)
     lax.fori_loop(1, 2, spread_core, 0)
     lax.fori_loop(last_late, n_z, add_x, 0)

time: 113 us -> 111 us (0.982)
  the two profiles are of different devices: /device:TPU:24 before, /device:TPU:0 now
where the time goes in v6:
time: 111 us; the launch traced here: 110 us
  Pallas kernels  106 us (95%)
  local copies, waits for them, and re-layouts  2.55 us (2%)
  between operations  1.29 us (1%)
    pallas_call x1, Pallas kernels, on_device(): pl.pallas_call(functools.partial(kernel, n_dp, n_rep), out_shape=(pltpu.V...  106 us
    unnamed x2, local copies, waits for them, and re-layouts  2.55 us

profile of v6, /device:TPU:0, one launch (start us, length us, event | category | flops | bytes accessed | tf_op | source)
XLA Modules:
  0.0 110.3 jit_solution(12671931240744747920)
XLA Ops:
  1.3 106.4 %shard_map.68 = (bf16[768,2048]{1,0:T(8,128)(2,1)S(1)}, f32[128,1536]{1,0:T(8,128)S(1)}) custom-call(s32[1]{0:T(128)S(6)} %copy.11.counts, bf16[768,1024]{1,0:T(8,128)(2,1)} %grad.1, bf16[768,1536]{1,0:T(8,128)(2,1)} %pre.1, bf16[1536,2048]{1,0:T(8,128)(2,1)} %up.1, bf16[2048,1536]{1,0:T(8,128)(2,1)} %down.1), custom_call_target="tpu_custom_call" | custom-call | tf_op jit(solution)/shard_map/pallas_call | solution.py:401
  107.7 1.7 %copy.9 = bf16[768,2048]{1,0:T(8,128)(2,1)} copy(bf16[768,2048]{1,0:T(8,128)(2,1)S(1)} %get-tuple-element.2) | data formatting | bytes 6291456
  109.4 0.9 copy.10

commit v7 on v6

--- a/solution.py
+++ b/solution.py
@@ -334,11 +334,11 @@
     lax.fori_loop(last_late, n_z, make_terms, 0)
     lax.fori_loop(last_late, n_z, add_core, 0)
     lax.fori_loop(2, 3, cross_x, 0)
+    lax.fori_loop(last_late, n_z, add_x, 0)
     lax.fori_loop(3, n_z, spread_z, 0)
     lax.fori_loop(3, n_z, cross_x, 0)
     pass_core(my_z)
     lax.fori_loop(1, 2, spread_core, 0)
-    lax.fori_loop(last_late, n_z, add_x, 0)
     lax.fori_loop(2, n_z, spread_core, 0)
     lax.fori_loop(0, n_z, spread_end, 0)
 

time: 111 us -> 111 us (level)
  no operation moved by 1% of the time
where the time goes in v7:
time: 111 us; the launch traced here: 110 us
  Pallas kernels  106 us (95%)
  local copies, waits for them, and re-layouts  2.55 us (2%)
  between operations  1.29 us (1%)
    pallas_call x1, Pallas kernels, on_device(): pl.pallas_call(functools.partial(kernel, n_dp, n_rep), out_shape=(pltpu.V...  106 us
    unnamed x2, local copies, waits for them, and re-layouts  2.55 us

profile of v7, /device:TPU:0, one launch (start us, length us, event | category | flops | bytes accessed | tf_op | source)
XLA Modules:
  0.0 110.3 jit_solution(14805717645202710123)
XLA Ops:
  1.3 106.4 %shard_map.68 = (bf16[768,2048]{1,0:T(8,128)(2,1)S(1)}, f32[128,1536]{1,0:T(8,128)S(1)}) custom-call(s32[1]{0:T(128)S(6)} %copy.11.counts, bf16[768,1024]{1,0:T(8,128)(2,1)} %grad.1, bf16[768,1536]{1,0:T(8,128)(2,1)} %pre.1, bf16[1536,2048]{1,0:T(8,128)(2,1)} %up.1, bf16[2048,1536]{1,0:T(8,128)(2,1)} %down.1), custom_call_target="tpu_custom_call" | custom-call | tf_op jit(solution)/shard_map/pallas_call | solution.py:401
  107.7 1.7 %copy.9 = bf16[768,2048]{1,0:T(8,128)(2,1)} copy(bf16[768,2048]{1,0:T(8,128)(2,1)S(1)} %get-tuple-element.2) | data formatting | bytes 6291456
  109.4 0.9 copy.10
